TPU v7x, 32 devices: a whole 2x2x4 slice. The times are simulated.
32 devices in a mesh: group: 2 (over y), scan: 4 (over z), tensor: 2 (over x), band: 2 (over core).
Axes of the slice: x: 2, y: 2, z: 4, core: 2. Of those that a mesh axis runs over, the one named last changes fastest.
Arguments:
- signal: bfloat16 [4096, 5120], P(('group', 'scan', 'band'), 'tensor'), parts along dimension 0, may hold values from -140 to 140
- gate_branch: bfloat16 [4096, 5120], P(('group', 'scan', 'band'), 'tensor'), parts along dimension 0, may hold values from -6 to 6
- write_proj: bfloat16 [4096, 128], P(('group', 'scan', 'band')), parts along dimension 0, may hold values from -1.796875 to 1.796875
- read_proj: bfloat16 [4096, 128], P(('group', 'scan', 'band')), parts along dimension 0, may hold values from -1.796875 to 1.796875
- step_logits: float32 [80, 4096], P('tensor', ('group', 'scan', 'band')), parts along dimension 1
- valid_mask: int32 [4096], P(('group', 'scan', 'band')), parts along dimension 0, may hold values from 0 to 1
- stretch_band: int32 [16], P(('group', 'scan', 'band')), parts along dimension 0, may hold values from 0 to 11
- band_offset: float32 [12, 80], P(None, 'tensor'), may hold values from -0.35 to 0.35
- decay_log: float32 [80], P('tensor'), may hold values from -8 to 0
- step_offset: float32 [80], P('tensor'), may hold values from -7 to -1
- skip_gain: float32 [80], P('tensor'), may hold values from 0.5 to 2
- norm_gain: float32 [5120], P('tensor'), may hold values from 0.1 to 1.9
- out_weight: bfloat16 [5120, 2560], P('tensor'), may hold values from -0.078125 to 0.078125
Outputs:
- layer_output: bfloat16 [4096, 2560], P(('group', 'scan', 'band'), 'tensor'), parts along dimension 0
There are 2 independent parts, one for each index of `group`. A program takes and returns all parts, laid end to end along the dimension named above; an argument that names none is the same for every part. Nothing has to cross between parts.
All inputs are finite; a program needn't handle non-finite values.
Results may differ from a plain program's by a relative error of at most 0.015.
Values may be sent and summed in bfloat16 or wider, within the bound.
A program may use at most 64 MiB of HBM per device.

v0:
```python
import jax
import jax.numpy as jnp
from jax import lax
from jax.sharding import PartitionSpec as P

HEAD_DIM = 64
STATE = 128
STRETCH = 256
BANDS = 12
INNER = 5120


EPSILON = 1e-05
HIGHEST = lax.Precision.HIGHEST


def step_sizes(step_logits, stretch_band, band_offset, step_offset):
    one_hot = (stretch_band[:, None] == jnp.arange(BANDS, dtype=jnp.int32)[None, :]).astype(
        jnp.float32
    )
    stretch_offset = jnp.dot(one_hot, band_offset, precision=HIGHEST)
    token_offset = jnp.repeat(stretch_offset, STRETCH, axis=0).T
    return jax.nn.softplus(step_logits + step_offset[:, None] + token_offset)


def combine(earlier, later_pair):
    return (
        earlier[0] + later_pair[0],
        jnp.exp(later_pair[0])[:, None, None] * earlier[1] + later_pair[1],
    )


def local_step(running_pair, member):
    return (combine(running_pair, member), running_pair)


def on_device(
    signal,
    gate_branch,
    write_proj,
    read_proj,
    step_logits,
    valid_mask,
    stretch_band,
    band_offset,
    decay_log,
    step_offset,
    skip_gain,
    norm_gain,
    out_weight,
):
    row_count = signal.shape[0]
    head_count = decay_log.shape[0]
    block_count = row_count // STRETCH
    step_size = step_sizes(step_logits, stretch_band, band_offset, step_offset)
    log_decay = step_size * (-jnp.exp(decay_log))[:, None]
    input_weight = step_size * valid_mask.astype(jnp.float32)[None, :]
    running = jnp.cumsum(log_decay.reshape(head_count, block_count, STRETCH), axis=2)
    weight_blocks = input_weight.reshape(head_count, block_count, STRETCH)
    signal_blocks = signal.reshape(block_count, STRETCH, head_count, HEAD_DIM)
    write_blocks = write_proj.reshape(block_count, STRETCH, STATE)
    read_blocks = read_proj.reshape(block_count, STRETCH, STATE)
    scores = jnp.einsum(
        "cin,cjn->cij", read_blocks, write_blocks, preferred_element_type=jnp.float32
    )
    lower_mask = jnp.arange(STRETCH)[:, None] >= jnp.arange(STRETCH)[None, :]
    span_logs = jnp.where(
        lower_mask[None, None], running[:, :, :, None] - running[:, :, None, :], -1e30
    )
    mixing = (jnp.exp(span_logs) * scores[None] * weight_blocks[:, :, None, :]).astype(jnp.bfloat16)
    local_out = jnp.einsum(
        "hcij,cjhp->cihp", mixing, signal_blocks, preferred_element_type=jnp.float32
    )
    tail_weight = jnp.exp(running[:, :, -1:] - running) * weight_blocks
    scaled = (
        signal_blocks.astype(jnp.float32) * jnp.transpose(tail_weight, (1, 2, 0))[:, :, :, None]
    ).astype(jnp.bfloat16)
    block_states = jnp.einsum(
        "cjhp,cjn->chpn", scaled, write_blocks, preferred_element_type=jnp.float32
    )
    block_decay = running[:, :, -1].T
    zero_state = jnp.zeros((head_count, HEAD_DIM, STATE), jnp.float32)
    zero_log = jnp.zeros((head_count,), jnp.float32)
    identity = (zero_log, zero_state)
    device_pair, segment_cumulative = lax.scan(local_step, identity, (block_decay, block_states))
    all_logs = lax.all_gather(device_pair[0][None], ("scan", "band"), axis=0, tiled=True)
    inclusive = jnp.cumsum(all_logs, axis=0)
    exclusive = inclusive - all_logs
    position = lax.axis_index(("scan", "band"))
    own_exclusive = lax.dynamic_index_in_dim(exclusive, position, 0, keepdims=False)
    shard_block = lax.all_gather(
        device_pair[1][None].astype(jnp.bfloat16), ("scan", "band"), axis=0, tiled=True
    ).astype(jnp.float32)
    how_many = shard_block.shape[0]
    sources = jnp.arange(how_many, dtype=jnp.int32)
    gap_logs = jnp.where((sources < position)[:, None], own_exclusive[None, :] - inclusive, -1e30)
    carry_state = zero_state + jnp.einsum(
        "kh,khpn->hpn", jnp.exp(gap_logs), shard_block, precision=HIGHEST
    )
    enter_state = (
        jnp.exp(segment_cumulative[0])[:, :, None, None] * carry_state[None] + segment_cumulative[1]
    )
    state_high = enter_state.astype(jnp.bfloat16)
    widened = lax.optimization_barrier(state_high).astype(jnp.float32)
    state_low = (enter_state - widened).astype(jnp.bfloat16)
    high_part = jnp.einsum(
        "cin,chpn->cihp", read_blocks, state_high, preferred_element_type=jnp.float32
    )
    low_part = jnp.einsum(
        "cin,chpn->cihp", read_blocks, state_low, preferred_element_type=jnp.float32
    )
    carried_out = jnp.transpose(jnp.exp(running), (1, 2, 0))[:, :, :, None] * (high_part + low_part)
    ssm_out = (local_out + carried_out).reshape(row_count, head_count, HEAD_DIM) + skip_gain[
        None, :, None
    ] * signal.reshape(row_count, head_count, HEAD_DIM).astype(jnp.float32)
    gated_out = ssm_out.reshape(row_count, head_count * HEAD_DIM) * jax.nn.silu(
        gate_branch.astype(jnp.float32)
    )
    square_total = lax.psum(jnp.sum(gated_out * gated_out, axis=1), "tensor")
    normed = (
        gated_out * lax.rsqrt(square_total / INNER + EPSILON)[:, None] * norm_gain[None, :]
    ).astype(jnp.bfloat16)
    own_columns = lax.psum_scatter(
        lax.dot_general(
            out_weight, normed, (((0,), (1,)), ((), ())), preferred_element_type=jnp.float32
        ).astype(jnp.bfloat16),
        "tensor",
        scatter_dimension=0,
        tiled=True,
    ).astype(jnp.float32)
    return own_columns.T.astype(jnp.bfloat16)


def solution(mesh):
    placed = (
        P(("group", "scan", "band"), "tensor"),
        P(("group", "scan", "band"), "tensor"),
        P(("group", "scan", "band"), None),
        P(("group", "scan", "band"), None),
        P("tensor", ("group", "scan", "band")),
        P(("group", "scan", "band")),
        P(("group", "scan", "band")),
        P(None, "tensor"),
        P("tensor"),
        P("tensor"),
        P("tensor"),
        P("tensor"),
        P("tensor", None),
    )
    return jax.shard_map(
        on_device,
        mesh=mesh,
        in_specs=placed,
        out_specs=P(("group", "scan", "band"), "tensor"),
        check_vma=False,
    )
```

profile of v0, /device:TPU:25, one launch (start us, length us, event | category | flops | bytes accessed | tf_op | source)
XLA Modules:
  0.0 132.0 jit_solution(8350640665615563211)
XLA Ops:
  7.2 0.7 exponential_negate_fusion
  7.9 0.8 convolution_bitcast_fusion
  8.7 0.9 broadcast_multiply_fusion.1
  9.6 0.6 reduce-window.6
  10.2 0.2 slice_reduce_fusion
  10.8 0.7 multiply_reduce_fusion.1
  11.5 0.7 convert_element_type.66
  12.2 1.6 %copy.39 = bf16[256,2560]{0,1:T(8,128)(2,1)S(1)} copy(bf16[256,2560]{1,0:T(8,128)(2,1)} %param.13) | data formatting | bytes 2621440 | tf_op args[0]
  14.0 0.3 fusion.10
  14.3 1.3 %fusion.16 = bf16[40,64,128]{2,1,0:T(8,128)(2,1)} fusion(bf16[256,40,64]{0,2,1:T(8,128)(2,1)S(1)} %bitcast.89, f32[40]{0:T(128)S(1)} %get-tuple-element.17, bf16[256,128]{1,0:T(8,128)(2,1)S(1)} %copy-done.4), kind=kOutput, calls=%fused_computation.27 | convolution fusion | flops 168427520 | bytes 2031776 | tf_op jit(solution)/shard_map/cjhp,cjn->chpn/dot_general | solution.py:78
  15.7 0.6 dynamic-slice.1
  17.0 0.2 dynamic-update-slice
  17.2 13.7 %all-reduce = f32[320]{0:T(512)S(1)} all-reduce(f32[320]{0:T(512)S(1)} %dynamic-update-slice), channel_id=2, replica_groups=mesh['group'=2,'scan'=4,'tensor'=2,'band'=2] {'scan','band'}, use_global_device_ids=true, to_apply=%add | all-reduce | flops 320 | bytes 2560
  31.2 1.4 %copy.42 = bf16[256,2560]{0,1:T(8,128)(2,1)} copy(bf16[256,2560]{1,0:T(8,128)(2,1)S(1)} %copy-done.3) | data formatting | bytes 2621440 | tf_op args[1]
  32.8 0.2 fusion.33
  33.0 37.8 %all-gather.4.cloned.1.call-done = bf16[320,64,128]{2,1,0:T(8,128)(2,1)} async-done(((bf16[40,64,128]{2,1,0:T(8,128)(2,1)}), bf16[320,64,128]{2,1,0:T(8,128)(2,1)}) %all-gather.4.cloned.1.call-update) | async-done | bytes 5242896 | tf_op jit(solution)/shard_map/all_gather | solution.py:91
  70.8 8.7 %fusion.1 = f32[40,1,64,128]{3,1,2,0:T(1,128)S(1)} fusion(f32[8,40,1,1]{0,2,3,1:T(1,128)S(1)} %copy.43, bf16[8,40,64,128]{3,2,1,0:T(8,128)(2,1)} %bitcast.88), kind=kOutput, calls=%fused_computation.2 | convolution fusion | flops 31457280 | bytes 6554880 | tf_op jit(solution)/shard_map/kh,khpn->hpn/dot_general | solution.py:97
  79.6 0.5 fusion.22
  80.1 0.5 fusion.20
  80.7 3.1 %bitcast_add_fusion = f32[1,256,40,64]{1,3,2,0:T(8,128)S(1)} fusion(f32[40,64,256]{2,1,0:T(8,128)S(1)} %fusion.22, f32[40,64,256]{2,1,0:T(8,128)S(1)} %fusion.20, bf16[256,40,64]{0,2,1:T(8,128)(2,1)S(1)} %bitcast.87, f32[40,256]{1,0:T(8,128)S(1)} %get-tuple-element.34, f32[256,256]{1,0:T(8,128)S(1)} %fusion.33, f32[40,256]{1,0:T(8,128)S(1)} %get-tuple-element.33, ...), kind=kOutput, calls=%fused_computation.22 | convolution fusion | flops 350617600 | bytes 9625600 | tf_op jit(solution)/shard_map/hcij,cjhp->cihp/dot_general | solution.py:71
  83.8 2.6 %multiply_reduce_fusion = (f32[256]{0:T(256)S(1)}, f32[256,2560]{0,1:T(8,128)S(1)}) fusion(bf16[256,2560]{0,1:T(8,128)(2,1)S(1)} %copy-done.2, bf16[256,2560]{0,1:T(8,128)(2,1)} %copy-done.1, f32[2560]{0:T(1024)S(1)} %mul.162, f32[1,256,40,64]{1,3,2,0:T(8,128)S(1)} %bitcast_add_fusion), kind=kLoop, calls=%fused_computation.25 | loop fusion | flops 7208704 | bytes 7875584 | tf_op jit(solution)/shard_map/reduce_sum | solution.py:119
  86.4 4.0 %psum.7 = f32[256]{0:T(256)S(1)} all-reduce(f32[256]{0:T(256)S(1)} %get-tuple-element.19), channel_id=1, replica_groups=mesh['group'=2,'scan'=4,'tensor'=2,'band'=2] {'tensor'}, use_global_device_ids=true, to_apply=%region_4.5 | all-reduce | flops 256 | bytes 2048 | tf_op jit(solution)/shard_map/psum | solution.py:119
  90.4 9.5 %fusion.9 = bf16[2560,256]{0,1:T(8,128)(2,1)} fusion(bf16[2560,2560]{1,0:T(8,128)(2,1)} %param.25, f32[256,2560]{0,1:T(8,128)S(1)} %get-tuple-element.20, f32[2560]{0:T(1024)S(1)} %copy-done.6, f32[256]{0:T(256)S(1)} %add_rsqrt_fusion), kind=kOutput, calls=%fused_computation.11 | convolution fusion | flops 3358064640 | bytes 17050624 | tf_op jit(solution)/shard_map/dot_general | solution.py:124
  99.9 25.3 %reduce-scatter.2.cloned.1.call-done = bf16[1280,256]{0,1:T(8,128)(2,1)} async-done(((bf16[2560,256]{0,1:T(8,128)(2,1)}), bf16[1280,256]{0,1:T(8,128)(2,1)}) %reduce-scatter.2.cloned.1.call-update) | async-done | bytes 655376 | tf_op jit(solution)/shard_map/reduce_scatter | solution.py:123
  (48 shorter events, 1.2 us)
Async XLA Ops:
  6.5 26.3 %copy-start = (bf16[256,128]{1,0:T(8,128)(2,1)S(1)}, bf16[256,128]{1,0:T(8,128)(2,1)}, u32[]{:S(2)}) copy-start(bf16[256,128]{1,0:T(8,128)(2,1)} %param.16) | copy-start | bytes 196612
  6.5 7.3 %copy-start.5 = (f32[40,256]{1,0:T(8,128)S(1)}, f32[40,256]{1,0:T(8,128)}, u32[]{:S(2)}) copy-start(f32[40,256]{1,0:T(8,128)} %param.17) | copy-start | bytes 122884
  6.5 7.3 %copy-start.7 = (f32[40]{0:T(128)S(1)}, f32[40]{0:T(128)}, u32[]{:S(2)}) copy-start(f32[40]{0:T(128)} %param.22) | copy-start | bytes 484
  6.5 64.3 %all-gather.4.cloned.1.call-start = ((), (), s32[]{:S(2)}) async-start(), calls=%async_computation.2 | async-start | bytes 5898240 | tf_op jit(solution)/shard_map/all_gather | solution.py:91
  12.2 2.1 %copy-start.4 = (bf16[256,128]{1,0:T(8,128)(2,1)S(1)}, bf16[256,128]{1,0:T(8,128)(2,1)}, u32[]{:S(2)}) copy-start(bf16[256,128]{1,0:T(8,128)(2,1)} %param.15) | copy-start | bytes 196612
  13.8 66.8 %copy-start.1 = (bf16[256,2560]{0,1:T(8,128)(2,1)}, bf16[256,2560]{0,1:T(8,128)(2,1)S(1)}, u32[]{:S(2)}) copy-start(bf16[256,2560]{0,1:T(8,128)(2,1)S(1)} %copy.39) | copy-start | bytes 3932164
  13.9 1.8 %copy-start.9 = (u32[32]{0:T(128)S(1)}, u32[32]{0:T(128)}, u32[]{:S(2)}) copy-start(u32[32]{0:T(128)} %constant.58) | copy-start | bytes 388
  14.0 17.2 %copy-start.3 = (bf16[256,2560]{1,0:T(8,128)(2,1)S(1)}, bf16[256,2560]{1,0:T(8,128)(2,1)}, u32[]{:S(2)}) copy-start(bf16[256,2560]{1,0:T(8,128)(2,1)} %param.14) | copy-start | bytes 3932164
  14.3 18.4 %copy-start.8 = (f32[40]{0:T(128)S(1)}, f32[40]{0:T(128)}, u32[]{:S(2)}) copy-start(f32[40]{0:T(128)} %param.23) | copy-start | bytes 484
  15.6 109.5 %reduce-scatter.2.cloned.1.call-start = ((), (), s32[]{:S(2)}) async-start(), calls=%async_computation.1 | async-start | bytes 1966080 | tf_op jit(solution)/shard_map/reduce_scatter | solution.py:123
  80.7 3.1 %copy-start.2 = (bf16[256,2560]{0,1:T(8,128)(2,1)S(1)}, bf16[256,2560]{0,1:T(8,128)(2,1)}, u32[]{:S(2)}) copy-start(bf16[256,2560]{0,1:T(8,128)(2,1)} %copy.42) | copy-start | bytes 3932164
  83.8 6.6 %copy-start.6 = (f32[2560]{0:T(1024)S(1)}, f32[2560]{0:T(1024)}, u32[]{:S(2)}) copy-start(f32[2560]{0:T(1024)} %param.24) | copy-start | bytes 30724
Sparse Core Ops, SparseCore 0:
  15.8 55.0 all-gather.3
  100.0 25.0 reduce-scatter.1
where the time goes:
time: 134 us; the launch traced here: 132 us
  waiting for transfers between devices  63.1 us (47%)
  matrix products  24.6 us (18%)
  blocking collectives  17.7 us (13%)
  between operations  15 us (11%)
  other arithmetic  6.85 us (5%)
  local copies, waits for them, and re-layouts  4.72 us (4%)
    all_gather x1, waiting for transfers between devices, on_device(): lax.all_gather(device_pair[1][None].astype(jnp.bfloat16), ('scan', 'band'...  37.8 us
    reduce_scatter x1, waiting for transfers between devices, on_device(): lax.psum_scatter(lax.dot_general(out_weight, normed, (((0,), (1,)), ((),...  25.3 us
    unnamed x1, blocking collectives  13.7 us
    dot_general x1, matrix products, on_device(): lax.dot_general(out_weight, normed, (((0,), (1,)), ((), ())), preferred_e...  9.46 us
    dot_general x1, matrix products, on_device(): jnp.einsum('kh,khpn->hpn', jnp.exp(gap_logs), shard_block, precision=HIGH...  8.66 us
    psum x1, blocking collectives, on_device(): square_total = lax.psum(jnp.sum(gated_out * gated_out, axis=1), 'tensor')  4 us
    unnamed x26, local copies, waits for them, and re-layouts  3.97 us
    dot_general x1, matrix products, on_device(): jnp.einsum('hcij,cjhp->cihp', mixing, signal_blocks, preferred_element_ty...  3.11 us
  transfers between devices with their start and end apart: 2, of which 2 were waited for; matrix products, arithmetic and copies ran while one was open for 2% of the time, Pallas kernels for 0%

commit v1 on v0

--- a/solution.py
+++ b/solution.py
@@ -1,6 +1,10 @@
+import functools
+
 import jax
 import jax.numpy as jnp
 from jax import lax
+from jax.experimental import pallas as pl
+from jax.experimental.pallas import tpu as pltpu
 from jax.sharding import PartitionSpec as P
 
 HEAD_DIM = 64
@@ -131,6 +135,421 @@
     return own_columns.T.astype(jnp.bfloat16)
 
 
+LOG2E = 1.4426950408889634
+LANES = 128
+PAIRS = 2
+TILE = 256
+MESH = pl.DeviceIdType.MESH
+
+
+def fused_kernel(
+    heads,
+    span_count,
+    band_count,
+    signal_ref,
+    gate_hbm,
+    write_ref,
+    read_ref,
+    logits_ref,
+    valid_ref,
+    band_ref,
+    offset_ref,
+    decay_ref,
+    bias_ref,
+    skip_ref,
+    gain_ref,
+    weight_hbm,
+    out_ref,
+    weight_ref,
+    gate_ref,
+    padded_ref,
+    params_ref,
+    row_ref,
+    spread_ref,
+    skip_rows_ref,
+    scores_ref,
+    read_by_token_ref,
+    run_ref,
+    lead_ref,
+    fed_ref,
+    state_ref,
+    total_ref,
+    local_ref,
+    normed_ref,
+    square_ref,
+    carry_ref,
+    pass_ref,
+    sent_ref,
+    landed_ref,
+    square_out_ref,
+    square_in_ref,
+    load_sem,
+    chain_send,
+    chain_recv,
+    tile_send,
+    tile_recv,
+    square_send,
+    square_recv,
+):
+    pair_count = heads // 2
+    chunk_count = pair_count // PAIRS
+    places = span_count * band_count
+    scan_index = lax.axis_index("scan")
+    band_index = lax.axis_index("band")
+    tensor_index = lax.axis_index("tensor")
+    place = scan_index * band_count + band_index
+    following = lax.rem(place + 1, places)
+    previous = lax.rem(place + places - 1, places)
+    peer = 1 - tensor_index
+
+    def at_place(spot):
+        return {"scan": spot // band_count, "band": lax.rem(spot, band_count)}
+
+    barrier = pltpu.get_barrier_semaphore()
+    for target in (at_place(following), at_place(previous), {"tensor": peer}):
+        pl.semaphore_signal(barrier, inc=1, device_id=target, device_id_type=MESH)
+    gate_load = pltpu.make_async_copy(gate_hbm, gate_ref, load_sem.at[0])
+    weight_load = pltpu.make_async_copy(weight_hbm, weight_ref, load_sem.at[1])
+    gate_load.start()
+    weight_load.start()
+
+    padded_ref[...] = jnp.zeros_like(padded_ref)
+    padded_ref[0:heads, :] = logits_ref[...]
+    params_ref[...] = jnp.zeros_like(params_ref)
+    chosen = lax.broadcasted_iota(jnp.int32, (BANDS, heads), 0) == band_ref[0]
+    params_ref[0:1, 0:heads] = bias_ref[...] + jnp.sum(
+        jnp.where(chosen, offset_ref[...], 0.0), axis=0, keepdims=True
+    )
+    params_ref[1:2, 0:heads] = jnp.exp(decay_ref[...])
+    params_ref[2:3, 0:heads] = skip_ref[...]
+    shifted = padded_ref[...].T + params_ref[0:1, :]
+    step_size = jnp.maximum(shifted, 0.0) + jnp.log1p(jnp.exp(-jnp.abs(shifted)))
+    lanes = lax.broadcasted_iota(jnp.int32, (STRETCH, LANES), 1)
+    tokens = lax.broadcasted_iota(jnp.int32, (STRETCH, LANES), 0)
+    real = lanes < heads
+    running = jnp.where(real, step_size * -params_ref[1:2, :], 0.0)
+    shift = 1
+    while shift < STRETCH:
+        running = running + jnp.where(tokens >= shift, pltpu.roll(running, shift, 0), 0.0)
+        shift *= 2
+    running = running * LOG2E
+    row_ref[...] = running.T
+    valid = jnp.broadcast_to(valid_ref[...].astype(jnp.float32), (LANES, STRETCH)).T
+    in_weight = jnp.where(real, step_size * valid, 0.0)
+
+    def three_parts(value):
+        high = value.astype(jnp.bfloat16).astype(jnp.float32)
+        rest = value - high
+        middle = rest.astype(jnp.bfloat16).astype(jnp.float32)
+        low = rest - middle
+        packed = high + pltpu.roll(middle, heads, 1) + pltpu.roll(low, 2 * heads, 1)
+        return packed.astype(jnp.bfloat16)
+
+    spread_ref[:, 0:LANES] = three_parts(running)
+    spread_ref[:, LANES : 2 * LANES] = three_parts(in_weight)
+    skip_rows_ref[...] = three_parts(jnp.broadcast_to(params_ref[2:3, :], (16, LANES)))
+    write_turned = write_ref[...].astype(jnp.float32).T.astype(jnp.bfloat16)
+    read_by_token_ref[...] = write_turned
+    scores = jnp.dot(read_ref[...], write_turned, preferred_element_type=jnp.float32)
+    square_rows = lax.broadcasted_iota(jnp.int32, (STRETCH, STRETCH), 0)
+    square_columns = lax.broadcasted_iota(jnp.int32, (STRETCH, STRETCH), 1)
+    scores_ref[...] = jnp.where(square_columns <= square_rows, scores, 0.0)
+    square_ref[...] = jnp.zeros_like(square_ref)
+
+    @pl.when(place == 0)
+    def _():
+        carry_ref[...] = jnp.zeros_like(carry_ref)
+
+    pl.semaphore_wait(barrier, 3)
+
+    def chain_copy(chunk):
+        return pltpu.make_async_remote_copy(
+            src_ref=pass_ref.at[chunk],
+            dst_ref=carry_ref.at[chunk],
+            send_sem=chain_send.at[chunk],
+            recv_sem=chain_recv.at[chunk],
+            device_id=at_place(following),
+            device_id_type=MESH,
+        )
+
+    def chain_step(chunk):
+        @pl.when(place > 0)
+        def _():
+            chain_copy(chunk).wait_recv()
+
+        @pl.when(place < places - 1)
+        def _():
+            for member in range(PAIRS):
+                pair = chunk * PAIRS + member
+                onward = (
+                    total_ref[pair][0:1, :] * carry_ref[chunk, member].astype(jnp.float32)
+                    + state_ref[pair]
+                )
+                pass_ref[chunk, member] = onward.astype(jnp.bfloat16)
+            chain_copy(chunk).start()
+
+    def columns_of(pair):
+        return pl.ds(pl.multiple_of(pair * LANES, LANES), LANES)
+
+    part = lax.broadcasted_iota(jnp.int32, (LANES, 2 * LANES), 0)
+    part = (
+        part
+        - jnp.where(part >= heads, heads, 0)
+        - jnp.where(part >= 2 * heads, heads, 0)
+    )
+    wide_side = lax.broadcasted_iota(jnp.int32, (LANES, 2 * LANES), 1) // LANES
+    wide_index = part - wide_side
+    narrow_side = lax.broadcasted_iota(jnp.int32, (LANES, LANES), 1) // HEAD_DIM
+    narrow_index = part[:, 0:LANES] - narrow_side
+    first_half = lanes < HEAD_DIM
+
+    def picker(index, pair):
+        return jnp.where(index == 2 * pair, 1.0, 0.0).astype(jnp.bfloat16)
+
+    def state_pair(pair):
+        columns = columns_of(pair)
+        both = jnp.dot(
+            spread_ref[:, 0:LANES], picker(wide_index, pair), preferred_element_type=jnp.float32
+        )
+        run_ref[pair] = both
+        weight = jnp.dot(
+            spread_ref[:, LANES : 2 * LANES],
+            picker(narrow_index, pair),
+            preferred_element_type=jnp.float32,
+        )
+        own_run = jnp.where(first_half, both[:, 0:LANES], both[:, LANES : 2 * LANES])
+        last_run = own_run[STRETCH - 1 : STRETCH, :]
+        fed = signal_ref[:, columns].astype(jnp.float32) * weight
+        fed_ref[:, columns] = fed.astype(jnp.bfloat16)
+        lead_ref[:, columns] = jnp.exp2(own_run)
+        scaled = (fed * jnp.exp2(last_run - own_run)).astype(jnp.bfloat16)
+        state_ref[pair] = jnp.dot(
+            read_by_token_ref[...], scaled, preferred_element_type=jnp.float32
+        )
+        total_ref[pair] = jnp.broadcast_to(jnp.exp2(last_run), (8, LANES))
+
+    def mix_pair(pair):
+        columns = columns_of(pair)
+        half = STRETCH // 2
+        tops, bottoms = [], []
+        fed = fed_ref[:, columns]
+        for side in range(2):
+            row = row_ref[pl.ds(2 * pair + side, 1), :]
+            run = run_ref[pair, :, side * LANES : (side + 1) * LANES]
+            near = jnp.exp2(jnp.minimum(run[0:half] - row[:, 0:half], 0.0))
+            far = jnp.exp2(jnp.minimum(run[half:] - row[:, 0:half], 0.0))
+            late = jnp.exp2(jnp.minimum(run[half:] - row[:, half:], 0.0))
+            near = (near * scores_ref[0:half, 0:half]).astype(jnp.bfloat16)
+            far = (far * scores_ref[half:, 0:half]).astype(jnp.bfloat16)
+            late = (late * scores_ref[half:, half:]).astype(jnp.bfloat16)
+            tops.append(jnp.dot(near, fed[0:half], preferred_element_type=jnp.float32))
+            bottoms.append(
+                jnp.dot(
+                    jnp.concatenate([far, late], axis=1), fed, preferred_element_type=jnp.float32
+                )
+            )
+        local_ref[0:half, columns] = jnp.where(first_half[0:half], tops[0], tops[1])
+        local_ref[half:, columns] = jnp.where(first_half[half:], bottoms[0], bottoms[1])
+
+    def gate_pair(chunk, member):
+        pair = chunk * PAIRS + member
+        columns = columns_of(pair)
+        carried = jnp.dot(
+            read_ref[...], carry_ref[chunk, member], preferred_element_type=jnp.float32
+        )
+        skip = jnp.dot(
+            skip_rows_ref[...], picker(narrow_index, pair), preferred_element_type=jnp.float32
+        )
+        ssm_out = (
+            local_ref[:, columns]
+            + lead_ref[:, columns] * carried
+            + skip[0:1, :] * signal_ref[:, columns].astype(jnp.float32)
+        )
+        gate = gate_ref[:, columns].astype(jnp.float32)
+        gated = ssm_out * (gate / (1.0 + jnp.exp(-gate)))
+        square_ref[...] += gated * gated
+        normed_ref[:, columns] = (gated * gain_ref[:, columns]).astype(jnp.bfloat16)
+
+    @pl.loop(0, chunk_count)
+    def _(chunk):
+        for member in range(PAIRS):
+            state_pair(chunk * PAIRS + member)
+
+        @pl.when(place == 0)
+        def _():
+            chain_step(chunk)
+
+    delay = jnp.minimum(chunk_count, (place * 3) // 2)
+
+    def chain_slot(slot):
+        chunk = slot - delay
+
+        @pl.when((place > 0) & (chunk >= 0) & (chunk < chunk_count))
+        def _():
+            chain_step(chunk)
+
+    @pl.loop(0, chunk_count)
+    def _(slot):
+        chain_slot(slot)
+        for member in range(PAIRS):
+            mix_pair(slot * PAIRS + member)
+
+    gate_load.wait()
+
+    @pl.loop(0, chunk_count)
+    def _(slot):
+        chain_slot(slot + chunk_count)
+        for member in range(PAIRS):
+            gate_pair(slot, member)
+
+    square_sum = jnp.sum(square_ref[...].T, axis=0, keepdims=True)
+    square_out_ref[...] = jnp.broadcast_to(square_sum, square_out_ref.shape)
+    square_copy = pltpu.make_async_remote_copy(
+        src_ref=square_out_ref,
+        dst_ref=square_in_ref,
+        send_sem=square_send,
+        recv_sem=square_recv,
+        device_id={"tensor": peer},
+        device_id_type=MESH,
+    )
+    square_copy.start()
+    weight_load.wait()
+    own_width = out_ref.shape[1]
+    tile_count = own_width // TILE
+
+    def tile_copy(tile):
+        return pltpu.make_async_remote_copy(
+            src_ref=sent_ref.at[tile],
+            dst_ref=landed_ref.at[tile],
+            send_sem=tile_send.at[tile],
+            recv_sem=tile_recv.at[tile],
+            device_id={"tensor": peer},
+            device_id_type=MESH,
+        )
+
+    def project(owner, tile):
+        start = pl.multiple_of(owner * own_width + tile * TILE, LANES)
+        return jnp.dot(
+            normed_ref[...], weight_ref[:, pl.ds(start, TILE)], preferred_element_type=jnp.float32
+        )
+
+    @pl.loop(0, tile_count)
+    def _(tile):
+        sent_ref[tile] = project(peer, tile).astype(jnp.bfloat16)
+        tile_copy(tile).start()
+
+    square_copy.wait()
+    inner = 2 * heads * HEAD_DIM
+    scale = lax.rsqrt((square_out_ref[0:1, :] + square_in_ref[0:1, :]) / inner + EPSILON)
+    square_ref[...] = jnp.broadcast_to(scale, (LANES, STRETCH)).T
+
+    @pl.loop(0, tile_count)
+    def _(tile):
+        own = project(tensor_index, tile)
+        tile_copy(tile).wait_recv()
+        both = own + landed_ref[tile].astype(jnp.float32)
+        scales = square_ref[...]
+        for side in range(TILE // LANES):
+            start = pl.multiple_of(tile * TILE + side * LANES, LANES)
+            out_ref[:, pl.ds(start, LANES)] = (
+                both[:, side * LANES : (side + 1) * LANES] * scales
+            ).astype(jnp.bfloat16)
+
+    @pl.loop(0, tile_count)
+    def _(tile):
+        tile_copy(tile).wait_send()
+
+    @pl.when(place < places - 1)
+    def _():
+        @pl.loop(0, chunk_count)
+        def _(chunk):
+            chain_copy(chunk).wait_send()
+
+
+def fused_on_device(
+    span_count,
+    band_count,
+    signal,
+    gate_branch,
+    write_proj,
+    read_proj,
+    step_logits,
+    valid_mask,
+    stretch_band,
+    band_offset,
+    decay_log,
+    step_offset,
+    skip_gain,
+    norm_gain,
+    out_weight,
+):
+    heads = decay_log.shape[0]
+    inner = heads * HEAD_DIM
+    width = out_weight.shape[1]
+    pair_count = heads // 2
+    chunk_count = pair_count // PAIRS
+    tile_count = width // 2 // TILE
+    vmem = pl.BlockSpec(memory_space=pltpu.VMEM)
+    hbm = pl.BlockSpec(memory_space=pl.ANY)
+    smem = pl.BlockSpec(memory_space=pltpu.SMEM)
+    f32, bf16 = jnp.float32, jnp.bfloat16
+    return pl.pallas_call(
+        functools.partial(fused_kernel, heads, span_count, band_count),
+        out_shape=jax.ShapeDtypeStruct((STRETCH, width // 2), bf16),
+        in_specs=[vmem, hbm] + [vmem] * 4 + [smem] + [vmem] * 5 + [hbm],
+        out_specs=vmem,
+        scratch_shapes=[
+            pltpu.VMEM((inner, width), bf16),
+            pltpu.VMEM((STRETCH, inner), bf16),
+            pltpu.VMEM((LANES, STRETCH), f32),
+            pltpu.VMEM((8, LANES), f32),
+            pltpu.VMEM((LANES, STRETCH), f32),
+            pltpu.VMEM((STRETCH, 2 * LANES), bf16),
+            pltpu.VMEM((16, LANES), bf16),
+            pltpu.VMEM((STRETCH, STRETCH), f32),
+            pltpu.VMEM((STATE, STRETCH), bf16),
+            pltpu.VMEM((pair_count, STRETCH, 2 * LANES), f32),
+            pltpu.VMEM((STRETCH, inner), f32),
+            pltpu.VMEM((STRETCH, inner), bf16),
+            pltpu.VMEM((pair_count, STATE, LANES), f32),
+            pltpu.VMEM((pair_count, 8, LANES), f32),
+            pltpu.VMEM((STRETCH, inner), f32),
+            pltpu.VMEM((STRETCH, inner), bf16),
+            pltpu.VMEM((STRETCH, LANES), f32),
+            pltpu.VMEM((chunk_count, PAIRS, STATE, LANES), bf16),
+            pltpu.VMEM((chunk_count, PAIRS, STATE, LANES), bf16),
+            pltpu.VMEM((tile_count, STRETCH, TILE), bf16),
+            pltpu.VMEM((tile_count, STRETCH, TILE), bf16),
+            pltpu.VMEM((8, STRETCH), f32),
+            pltpu.VMEM((8, STRETCH), f32),
+            pltpu.SemaphoreType.DMA((2,)),
+            pltpu.SemaphoreType.DMA((chunk_count,)),
+            pltpu.SemaphoreType.DMA((chunk_count,)),
+            pltpu.SemaphoreType.DMA((tile_count,)),
+            pltpu.SemaphoreType.DMA((tile_count,)),
+            pltpu.SemaphoreType.DMA,
+            pltpu.SemaphoreType.DMA,
+        ],
+        compiler_params=pltpu.CompilerParams(
+            collective_id=0, has_side_effects=True, vmem_limit_bytes=60 * 1024 * 1024
+        ),
+    )(
+        signal,
+        gate_branch,
+        write_proj,
+        read_proj,
+        step_logits,
+        valid_mask[None, :],
+        stretch_band,
+        band_offset,
+        decay_log[None, :],
+        step_offset[None, :],
+        skip_gain[None, :],
+        norm_gain[None, :],
+        out_weight,
+    )
+
+
 def solution(mesh):
     placed = (
         P(("group", "scan", "band"), "tensor"),
@@ -147,10 +566,33 @@
         P("tensor"),
         P("tensor", None),
     )
-    return jax.shard_map(
-        on_device,
-        mesh=mesh,
-        in_specs=placed,
-        out_specs=P(("group", "scan", "band"), "tensor"),
-        check_vma=False,
-    )
+    shape = dict(mesh.shape)
+    places = shape["scan"] * shape["band"]
+
+    def layer(*arrays):
+        rows = arrays[0].shape[0] // (shape["group"] * places)
+        heads = arrays[8].shape[0] // shape["tensor"]
+        width = arrays[12].shape[1]
+        fits = (
+            shape["tensor"] == 2
+            and places > 2
+            and rows == STRETCH
+            and heads % (2 * PAIRS) == 0
+            and 3 * heads <= LANES
+            and width % (2 * TILE) == 0
+        )
+        member = on_device
+        if fits:
+            member = functools.partial(fused_on_device, shape["scan"], shape["band"])
+        return mapped(member)(*arrays)
+
+    def mapped(member):
+        return jax.shard_map(
+            member,
+            mesh=mesh,
+            in_specs=placed,
+            out_specs=P(("group", "scan", "band"), "tensor"),
+            check_vma=False,
+        )
+
+    return layer

time: 134 us -> 48.3 us (0.36); the launches traced: 132 us -> 48.1 us
  waiting for transfers between devices: 63.1 us -> 0 us
  Pallas kernels: 0 us -> 44.1 us
  matrix products: 24.6 us -> 0 us
  blocking collectives: 17.7 us -> 0 us
  between operations: 15 us -> 0.66 us
  other arithmetic: 6.85 us -> 0 us
  local copies, waits for them, and re-layouts: 4.72 us -> 3.28 us
    pallas_call x0 -> x1, Pallas kernels: none -> 44.1 us  [fused_on_device(): pl.pallas_call(functools.partial(fused_kernel, heads, span_count, band_co...]
    all_gather x1 -> x0, waiting for transfers between devices: 37.8 us -> none  [on_device(): lax.all_gather(device_pair[1][None].astype(jnp.bfloat16), ('scan', 'band'...]
    reduce_scatter x1 -> x0, waiting for transfers between devices: 25.3 us -> none  [on_device(): lax.psum_scatter(lax.dot_general(out_weight, normed, (((0,), (1,)), ((),...]
    dot_general x8 -> x0, matrix products: 24.6 us -> none  [the longest x1 9.46 us: on_device(): lax.dot_general(out_weight, normed, (((0,), (1,)), ((), ())), preferred_e...]
    unnamed x1 -> x0, blocking collectives: 13.7 us -> none
    psum x1 -> x0, blocking collectives: 4 us -> none  [on_device(): square_total = lax.psum(jnp.sum(gated_out * gated_out, axis=1), 'tensor')]
    reduce_sum x1 -> x0, other arithmetic: 2.58 us -> none  [on_device(): square_total = lax.psum(jnp.sum(gated_out * gated_out, axis=1), 'tensor')]
    unnamed x26 -> x1, local copies, waits for them, and re-layouts: 3.97 us -> 1.97 us
  transfers between devices with their start and end apart: 2 -> 0, of which waited for: 2 -> 0; matrix products, arithmetic and copies ran while one was open for 2% -> 0% of each run, Pallas kernels for 0% -> 0%
where the time goes in v1:
time: 48.3 us; the launch traced here: 48.1 us
  Pallas kernels  44.1 us (91%)
  local copies, waits for them, and re-layouts  3.28 us (7%)
  between operations  0.66 us (1%)
    pallas_call x1, Pallas kernels, fused_on_device(): pl.pallas_call(functools.partial(fused_kernel, heads, span_count, band_co...  44.1 us
    unnamed x1, local copies, waits for them, and re-layouts  1.97 us
    broadcast_in_dim x1, local copies, waits for them, and re-layouts, fused_on_device(): norm_gain[None, :]  1.31 us

profile of v1, /device:TPU:25, one launch (start us, length us, event | category | flops | bytes accessed | tf_op | source)
XLA Modules:
  0.0 48.1 jit_solution(946453939830910065)
XLA Ops:
  0.7 1.3 %broadcast_in_dim.19.gain_ref = f32[1,2560]{1,0:T(1,128)} reshape(f32[2560]{0:T(1024)} %param.24) | data formatting | bytes 20480 | tf_op jit(solution)/shard_map/broadcast_in_dim | solution.py:548
  2.0 44.1 %shard_map.127 = bf16[256,1280]{1,0:T(8,128)(2,1)} custom-call(bf16[256,2560]{1,0:T(8,128)(2,1)} %signal_ref.1, bf16[256,2560]{1,0:T(8,128)(2,1)} %gate_hbm.1, bf16[256,128]{1,0:T(8,128)(2,1)} %write_ref.1, bf16[256,128]{1,0:T(8,128)(2,1)} %read_ref.1, f32[40,256]{1,0:T(8,128)} %logits_ref.1, s32[1,256]{1,0:T(1,128)} %bitcast.4, s32[1]{0:T(128)S(6)} %copy.15.band_ref, ...), custom_call_target="tpu_custom_call" | custom-call | tf_op jit(solution)/shard_map/pallas_call | solution.py:496
  46.1 2.0 %copy.16 = bf16[256,1280]{1,0:T(8,128)(2,1)} copy(bf16[256,1280]{1,0:T(8,128)(2,1)} %shard_map.127) | data formatting | bytes 1310720

commit v2 on v1

--- a/solution.py
+++ b/solution.py
@@ -137,7 +137,8 @@
 
 LOG2E = 1.4426950408889634
 LANES = 128
-PAIRS = 2
+PAIRS = 1
+GROUP = 4
 TILE = 256
 MESH = pl.DeviceIdType.MESH
 
@@ -169,7 +170,6 @@
     skip_rows_ref,
     scores_ref,
     read_by_token_ref,
-    run_ref,
     lead_ref,
     fed_ref,
     state_ref,
@@ -301,6 +301,14 @@
     wide_index = part - wide_side
     narrow_side = lax.broadcasted_iota(jnp.int32, (LANES, LANES), 1) // HEAD_DIM
     narrow_index = part[:, 0:LANES] - narrow_side
+    outside = jnp.full((LANES, LANES), -1, jnp.int32)
+    block_index = jnp.concatenate(
+        [
+            jnp.concatenate([narrow_index, outside], axis=1),
+            jnp.concatenate([outside, narrow_index], axis=1),
+        ],
+        axis=0,
+    )
     first_half = lanes < HEAD_DIM
 
     def picker(index, pair):
@@ -309,15 +317,10 @@
     def state_pair(pair):
         columns = columns_of(pair)
         both = jnp.dot(
-            spread_ref[:, 0:LANES], picker(wide_index, pair), preferred_element_type=jnp.float32
-        )
-        run_ref[pair] = both
-        weight = jnp.dot(
-            spread_ref[:, LANES : 2 * LANES],
-            picker(narrow_index, pair),
-            preferred_element_type=jnp.float32,
-        )
-        own_run = jnp.where(first_half, both[:, 0:LANES], both[:, LANES : 2 * LANES])
+            spread_ref[...], picker(block_index, pair), preferred_element_type=jnp.float32
+        )
+        own_run = both[:, 0:LANES]
+        weight = both[:, LANES : 2 * LANES]
         last_run = own_run[STRETCH - 1 : STRETCH, :]
         fed = signal_ref[:, columns].astype(jnp.float32) * weight
         fed_ref[:, columns] = fed.astype(jnp.bfloat16)
@@ -333,9 +336,12 @@
         half = STRETCH // 2
         tops, bottoms = [], []
         fed = fed_ref[:, columns]
+        runs = jnp.dot(
+            spread_ref[:, 0:LANES], picker(wide_index, pair), preferred_element_type=jnp.float32
+        )
         for side in range(2):
             row = row_ref[pl.ds(2 * pair + side, 1), :]
-            run = run_ref[pair, :, side * LANES : (side + 1) * LANES]
+            run = runs[:, side * LANES : (side + 1) * LANES]
             near = jnp.exp2(jnp.minimum(run[0:half] - row[:, 0:half], 0.0))
             far = jnp.exp2(jnp.minimum(run[half:] - row[:, 0:half], 0.0))
             late = jnp.exp2(jnp.minimum(run[half:] - row[:, half:], 0.0))
@@ -368,18 +374,19 @@
         gate = gate_ref[:, columns].astype(jnp.float32)
         gated = ssm_out * (gate / (1.0 + jnp.exp(-gate)))
         square_ref[...] += gated * gated
-        normed_ref[:, columns] = (gated * gain_ref[:, columns]).astype(jnp.bfloat16)
-
-    @pl.loop(0, chunk_count)
-    def _(chunk):
-        for member in range(PAIRS):
-            state_pair(chunk * PAIRS + member)
+        normed_ref[:, columns] = (gated * gain_ref[pl.ds(pair, 1), :]).astype(jnp.bfloat16)
+
+    @pl.loop(0, chunk_count // GROUP)
+    def _(group):
+        for member in range(GROUP * PAIRS):
+            state_pair(group * GROUP * PAIRS + member)
 
         @pl.when(place == 0)
         def _():
-            chain_step(chunk)
-
-    delay = jnp.minimum(chunk_count, (place * 3) // 2)
+            for member in range(GROUP):
+                chain_step(group * GROUP + member)
+
+    delay = jnp.minimum(chunk_count, place * 6)
 
     def chain_slot(slot):
         chunk = slot - delay
@@ -495,7 +502,7 @@
     f32, bf16 = jnp.float32, jnp.bfloat16
     return pl.pallas_call(
         functools.partial(fused_kernel, heads, span_count, band_count),
-        out_shape=jax.ShapeDtypeStruct((STRETCH, width // 2), bf16),
+        out_shape=pltpu.VMEM((STRETCH, width // 2), bf16),
         in_specs=[vmem, hbm] + [vmem] * 4 + [smem] + [vmem] * 5 + [hbm],
         out_specs=vmem,
         scratch_shapes=[
@@ -508,7 +515,6 @@
             pltpu.VMEM((16, LANES), bf16),
             pltpu.VMEM((STRETCH, STRETCH), f32),
             pltpu.VMEM((STATE, STRETCH), bf16),
-            pltpu.VMEM((pair_count, STRETCH, 2 * LANES), f32),
             pltpu.VMEM((STRETCH, inner), f32),
             pltpu.VMEM((STRETCH, inner), bf16),
             pltpu.VMEM((pair_count, STATE, LANES), f32),
@@ -545,7 +551,7 @@
         decay_log[None, :],
         step_offset[None, :],
         skip_gain[None, :],
-        norm_gain[None, :],
+        norm_gain.reshape(pair_count, LANES),
         out_weight,
     )
 
@@ -577,7 +583,7 @@
             shape["tensor"] == 2
             and places > 2
             and rows == STRETCH
-            and heads % (2 * PAIRS) == 0
+            and heads % (2 * PAIRS * GROUP) == 0
             and 3 * heads <= LANES
             and width % (2 * TILE) == 0
         )

time: 48.3 us -> 46.5 us (0.963)
  local copies, waits for them, and re-layouts: 3.28 us -> 0.84 us
  Pallas kernels: 44.1 us -> 44.8 us
    broadcast_in_dim x1 -> x0, local copies, waits for them, and re-layouts: 1.31 us -> none  [fused_on_device(): norm_gain[None, :]]
    unnamed x1, local copies, waits for them, and re-layouts: 1.97 us -> 0.84 us
    pallas_call x1, Pallas kernels: 44.1 us -> 44.8 us  [fused_on_device(): pl.pallas_call(functools.partial(fused_kernel, heads, span_count, band_co...]
where the time goes in v2:
time: 46.5 us; the launch traced here: 46.3 us
  Pallas kernels  44.8 us (96%)
  local copies, waits for them, and re-layouts  0.84 us (2%)
  between operations  0.66 us (1%)
    pallas_call x1, Pallas kernels, fused_on_device(): pl.pallas_call(functools.partial(fused_kernel, heads, span_count, band_co...  44.8 us

profile of v2, /device:TPU:25, one launch (start us, length us, event | category | flops | bytes accessed | tf_op | source)
XLA Modules:
  0.0 46.3 jit_solution(12784671341061543296)
XLA Ops:
  0.7 44.8 %shard_map.127 = bf16[256,1280]{1,0:T(8,128)(2,1)S(1)} custom-call(bf16[256,2560]{1,0:T(8,128)(2,1)} %signal_ref.1, bf16[256,2560]{1,0:T(8,128)(2,1)} %gate_hbm.1, bf16[256,128]{1,0:T(8,128)(2,1)} %write_ref.1, bf16[256,128]{1,0:T(8,128)(2,1)} %read_ref.1, f32[40,256]{1,0:T(8,128)} %logits_ref.1, s32[1,256]{1,0:T(1,128)} %bitcast.6, s32[1]{0:T(128)S(6)} %copy.16.band_ref, ...), custom_call_target="tpu_custom_call" | custom-call | tf_op jit(solution)/shard_map/pallas_call | solution.py:503
  45.5 0.8 %copy.15 = bf16[256,1280]{1,0:T(8,128)(2,1)} copy(bf16[256,1280]{1,0:T(8,128)(2,1)S(1)} %shard_map.127) | data formatting | bytes 1310720

commit v3 on v2

--- a/solution.py
+++ b/solution.py
@@ -137,8 +137,11 @@
 
 LOG2E = 1.4426950408889634
 LANES = 128
-PAIRS = 1
-GROUP = 4
+PAIRS = 2
+STATE_PAIRS = 4
+MIX_PAIRS = 4
+GATE_PAIRS = 2
+SLOTS = 2
 TILE = 256
 MESH = pl.DeviceIdType.MESH
 
@@ -147,7 +150,7 @@
     heads,
     span_count,
     band_count,
-    signal_ref,
+    signal_hbm,
     gate_hbm,
     write_ref,
     read_ref,
@@ -162,6 +165,7 @@
     weight_hbm,
     out_ref,
     weight_ref,
+    signal_ref,
     gate_ref,
     padded_ref,
     params_ref,
@@ -208,8 +212,10 @@
     barrier = pltpu.get_barrier_semaphore()
     for target in (at_place(following), at_place(previous), {"tensor": peer}):
         pl.semaphore_signal(barrier, inc=1, device_id=target, device_id_type=MESH)
+    signal_load = pltpu.make_async_copy(signal_hbm, signal_ref, load_sem.at[2])
     gate_load = pltpu.make_async_copy(gate_hbm, gate_ref, load_sem.at[0])
     weight_load = pltpu.make_async_copy(weight_hbm, weight_ref, load_sem.at[1])
+    signal_load.start()
     gate_load.start()
     weight_load.start()
 
@@ -260,6 +266,7 @@
     def _():
         carry_ref[...] = jnp.zeros_like(carry_ref)
 
+    signal_load.wait()
     pl.semaphore_wait(barrier, 3)
 
     def chain_copy(chunk):
@@ -373,20 +380,20 @@
         )
         gate = gate_ref[:, columns].astype(jnp.float32)
         gated = ssm_out * (gate / (1.0 + jnp.exp(-gate)))
-        square_ref[...] += gated * gated
         normed_ref[:, columns] = (gated * gain_ref[pl.ds(pair, 1), :]).astype(jnp.bfloat16)
-
-    @pl.loop(0, chunk_count // GROUP)
+        return gated * gated
+
+    @pl.loop(0, pair_count // STATE_PAIRS)
     def _(group):
-        for member in range(GROUP * PAIRS):
-            state_pair(group * GROUP * PAIRS + member)
+        for member in range(STATE_PAIRS):
+            state_pair(group * STATE_PAIRS + member)
 
         @pl.when(place == 0)
         def _():
-            for member in range(GROUP):
-                chain_step(group * GROUP + member)
-
-    delay = jnp.minimum(chunk_count, place * 6)
+            for member in range(STATE_PAIRS // PAIRS):
+                chain_step(group * (STATE_PAIRS // PAIRS) + member)
+
+    delay = jnp.minimum(chunk_count, place * SLOTS)
 
     def chain_slot(slot):
         chunk = slot - delay
@@ -395,19 +402,25 @@
         def _():
             chain_step(chunk)
 
-    @pl.loop(0, chunk_count)
-    def _(slot):
-        chain_slot(slot)
-        for member in range(PAIRS):
-            mix_pair(slot * PAIRS + member)
+    @pl.loop(0, pair_count // MIX_PAIRS)
+    def _(group):
+        for member in range(MIX_PAIRS // PAIRS):
+            chain_slot(group * (MIX_PAIRS // PAIRS) + member)
+        for member in range(MIX_PAIRS):
+            mix_pair(group * MIX_PAIRS + member)
 
     gate_load.wait()
 
-    @pl.loop(0, chunk_count)
-    def _(slot):
-        chain_slot(slot + chunk_count)
-        for member in range(PAIRS):
-            gate_pair(slot, member)
+    @pl.loop(0, pair_count // GATE_PAIRS)
+    def _(group):
+        for member in range(GATE_PAIRS // PAIRS):
+            chain_slot(chunk_count + group * (GATE_PAIRS // PAIRS) + member)
+        squares = square_ref[...]
+        for member in range(GATE_PAIRS):
+            squares = squares + gate_pair(
+                group * (GATE_PAIRS // PAIRS) + member // PAIRS, member % PAIRS
+            )
+        square_ref[...] = squares
 
     square_sum = jnp.sum(square_ref[...].T, axis=0, keepdims=True)
     square_out_ref[...] = jnp.broadcast_to(square_sum, square_out_ref.shape)
@@ -503,10 +516,11 @@
     return pl.pallas_call(
         functools.partial(fused_kernel, heads, span_count, band_count),
         out_shape=pltpu.VMEM((STRETCH, width // 2), bf16),
-        in_specs=[vmem, hbm] + [vmem] * 4 + [smem] + [vmem] * 5 + [hbm],
+        in_specs=[hbm, hbm] + [vmem] * 4 + [smem] + [vmem] * 5 + [hbm],
         out_specs=vmem,
         scratch_shapes=[
             pltpu.VMEM((inner, width), bf16),
+            pltpu.VMEM((STRETCH, inner), bf16),
             pltpu.VMEM((STRETCH, inner), bf16),
             pltpu.VMEM((LANES, STRETCH), f32),
             pltpu.VMEM((8, LANES), f32),
@@ -528,7 +542,7 @@
             pltpu.VMEM((tile_count, STRETCH, TILE), bf16),
             pltpu.VMEM((8, STRETCH), f32),
             pltpu.VMEM((8, STRETCH), f32),
-            pltpu.SemaphoreType.DMA((2,)),
+            pltpu.SemaphoreType.DMA((3,)),
             pltpu.SemaphoreType.DMA((chunk_count,)),
             pltpu.SemaphoreType.DMA((chunk_count,)),
             pltpu.SemaphoreType.DMA((tile_count,)),
@@ -583,7 +597,9 @@
             shape["tensor"] == 2
             and places > 2
             and rows == STRETCH
-            and heads % (2 * PAIRS * GROUP) == 0
+            and heads % (2 * STATE_PAIRS) == 0
+            and heads % (2 * MIX_PAIRS) == 0
+            and heads % (2 * GATE_PAIRS) == 0
             and 3 * heads <= LANES
             and width % (2 * TILE) == 0
         )

time: 46.5 us -> 44.3 us (0.953)
  Pallas kernels: 44.8 us -> 42.6 us
    pallas_call x1, Pallas kernels: 44.8 us -> 42.6 us  [fused_on_device(): pl.pallas_call(functools.partial(fused_kernel, heads, span_count, band_co...]
where the time goes in v3:
time: 44.3 us; the launch traced here: 44.1 us
  Pallas kernels  42.6 us (96%)
  local copies, waits for them, and re-layouts  0.84 us (2%)
  between operations  0.66 us (1%)
    pallas_call x1, Pallas kernels, fused_on_device(): pl.pallas_call(functools.partial(fused_kernel, heads, span_count, band_co...  42.6 us

profile of v3, /device:TPU:25, one launch (start us, length us, event | category | flops | bytes accessed | tf_op | source)
XLA Modules:
  0.0 44.1 jit_solution(10130191316884810613)
XLA Ops:
  0.7 42.6 %shard_map.127 = bf16[256,1280]{1,0:T(8,128)(2,1)S(1)} custom-call(bf16[256,2560]{1,0:T(8,128)(2,1)} %signal_hbm.1, bf16[256,2560]{1,0:T(8,128)(2,1)} %gate_hbm.1, bf16[256,128]{1,0:T(8,128)(2,1)} %write_ref.1, bf16[256,128]{1,0:T(8,128)(2,1)} %read_ref.1, f32[40,256]{1,0:T(8,128)} %logits_ref.1, s32[1,256]{1,0:T(1,128)} %bitcast.6, s32[1]{0:T(128)S(6)} %copy.16.band_ref, ...), custom_call_target="tpu_custom_call" | custom-call | tf_op jit(solution)/shard_map/pallas_call | solution.py:516
  43.3 0.8 %copy.15 = bf16[256,1280]{1,0:T(8,128)(2,1)} copy(bf16[256,1280]{1,0:T(8,128)(2,1)S(1)} %shard_map.127) | data formatting | bytes 1310720
